TPU v7x, 32 devices: a whole 2x2x4 slice. The times are simulated.
32 devices in a mesh: gx: 4 (over x, core), gy: 8 (over z, y).
Axes of the slice: x: 2, y: 2, z: 4, core: 2. Of those that a mesh axis runs over, the one named last changes fastest.
Arguments:
- patches: bfloat16 [4096, 1664], P('gy', 'gx'), may hold values from -6 to 6
- segment_ids: int32 [4096], P('gy'), may hold values from 0 to 31, as said below
- image_requests: int32 [32], replicated, may hold values from 0 to 7
- merge_index: int32 [1024, 4], P('gy'), may hold values from 0 to 4095, as said below
- qkv_weight: bfloat16 [1664, 3, 1664], P('gy', None, 'gx'), may hold values from -128 to 128
- out_weight: bfloat16 [1664, 1664], P('gx', 'gy'), may hold values from -0.15625 to 0.15625
- up_weight: bfloat16 [1664, 8192], P('gy', 'gx'), may hold values from -0.15625 to 0.15625
- down_weight: bfloat16 [8192, 1664], P('gx', 'gy'), may hold values from -0.0625 to 0.0625
- merge_weight: bfloat16 [6656, 4096], P('gy', 'gx'), may hold values from -0.078125 to 0.078125
Outputs:
- merged: bfloat16 [1024, 4096], P('gy', 'gx')
- request_norms: float32 [8], replicated
- top_logit: float32 [], replicated
Inputs may be any that keep to these rules, and one draw needn't show every extreme that they name: `segment_ids`: segment ids never fall along the tokens; the 512 tokens of block b (tokens b * 512 onward) hold exactly the images b * 4 to (b + 1) * 4 - 1, each a multiple of 4 tokens long. `merge_index`: every token stands in exactly one merged row; the four tokens of merged row m belong to one image, in the block of 512 tokens that holds token 4 * m.
All inputs are finite; a program needn't handle non-finite values.
Results may differ from a plain program's by a relative error of at most 0.011.
Values may be sent and summed in bfloat16 or wider, within the bound.
A program may use at most 128 MiB of HBM per device.

v0:
```python
import math
import jax
import jax.numpy as jnp
from jax import lax
from jax.sharding import PartitionSpec as P

HEAD = 104
IMG_GRP = 4


def layer_norm(values):
    center = jnp.mean(values, axis=-1, keepdims=True)
    square = jnp.mean(values * values, axis=-1, keepdims=True)
    return (values - center) * lax.rsqrt(square - center * center + 1e-06)


def add_columns(left, piece):
    flat = piece.reshape(piece.shape[0], -1)
    return jnp.dot(left, flat, preferred_element_type=jnp.float32)


def finish_sum(head_partial, stream_full, feat_share):
    own_index = lax.axis_index("gx")
    summed = lax.psum(head_partial, "gx")
    new_full = (stream_full.astype(jnp.float32) + summed).astype(jnp.bfloat16)
    new_share = lax.dynamic_slice_in_dim(new_full, own_index * feat_share, feat_share, 1)
    return (new_full, new_share)


def per_device(
    patches,
    segment_ids,
    image_requests,
    merge_index,
    qkv_weight,
    out_weight,
    up_weight,
    down_weight,
    merge_weight,
):
    tok_rows = patches.shape[0]
    feat_share = patches.shape[1]
    group_index = lax.axis_index("gy")
    stream_full = lax.all_gather(patches, "gx", axis=1, tiled=True)
    normed = layer_norm(stream_full.astype(jnp.float32)).astype(jnp.bfloat16)
    head_share = qkv_weight.shape[2]
    local_heads = head_share // HEAD
    projected = add_columns(normed, lax.all_gather(qkv_weight, "gy", axis=0, tiled=True))
    projected = projected.astype(jnp.bfloat16).reshape(tok_rows, 3, local_heads, HEAD)
    scores = jnp.einsum(
        "qhe,khe->hqk", projected[:, 0], projected[:, 1], preferred_element_type=jnp.float32
    ) / math.sqrt(HEAD)
    allowed = segment_ids[:, None] == segment_ids[None, :]
    scores = jnp.where(allowed[None], scores, -1e30)
    probs = jax.nn.softmax(scores, axis=-1).astype(jnp.bfloat16)
    mixed = jnp.einsum("hqk,khe->qhe", probs, projected[:, 2], preferred_element_type=jnp.float32)
    mixed = mixed.astype(jnp.bfloat16).reshape(tok_rows, head_share)
    head_partial = jnp.dot(
        mixed,
        lax.all_gather(out_weight, "gy", axis=1, tiled=True),
        preferred_element_type=jnp.float32,
    )
    stream_full, stream_share = finish_sum(head_partial, stream_full, feat_share)
    normed_two = layer_norm(stream_full.astype(jnp.float32)).astype(jnp.bfloat16)
    hidden = add_columns(normed_two, lax.all_gather(up_weight, "gy", axis=0, tiled=True))
    hidden = jax.nn.gelu(hidden, approximate=False).astype(jnp.bfloat16)
    unit_partial = jnp.dot(
        hidden,
        lax.all_gather(down_weight, "gy", axis=1, tiled=True),
        preferred_element_type=jnp.float32,
    )
    final_full, final_share = finish_sum(unit_partial, stream_full, feat_share)
    row_squares = jnp.sum(jnp.square(final_share.astype(jnp.float32)), axis=1)
    image_ids = group_index * IMG_GRP + jnp.arange(IMG_GRP, dtype=jnp.int32)
    member = segment_ids[:, None] == image_ids[None, :]
    image_sq = jnp.sum(jnp.where(member, row_squares[:, None], 0.0), axis=0)
    local_requests = lax.dynamic_slice_in_dim(image_requests, group_index * IMG_GRP, IMG_GRP)
    request_count = image_requests.shape[0] // 4
    owner = local_requests[:, None] == jnp.arange(request_count, dtype=jnp.int32)[None, :]
    request_part = jnp.sum(jnp.where(owner, image_sq[:, None], 0.0), axis=0)
    local_index = (merge_index - group_index * tok_rows).reshape(-1)
    joined = jnp.take(final_full, local_index, axis=0).reshape(
        merge_index.shape[0], 4 * final_full.shape[1]
    )
    logits = add_columns(joined, lax.all_gather(merge_weight, "gy", axis=0, tiled=True))
    local_top = jnp.max(logits)
    request_sq = lax.psum(request_part, ("gx", "gy"))
    top_logit = lax.pmax(local_top, ("gx", "gy"))
    return (logits.astype(jnp.bfloat16), jnp.sqrt(request_sq), top_logit)


def solution(mesh):
    in_specs = (
        P("gy", "gx"),
        P("gy"),
        P(),
        P("gy", None),
        P("gy", None, "gx"),
        P("gx", "gy"),
        P("gy", "gx"),
        P("gx", "gy"),
        P("gy", "gx"),
    )
    out_specs = (P("gy", "gx"), P(), P())
    return jax.shard_map(
        per_device, mesh=mesh, in_specs=in_specs, out_specs=out_specs, check_vma=False
    )
```

profile of v0, /device:TPU:0, one launch (start us, length us, event | category | flops | bytes accessed | tf_op | source)
XLA Modules:
  0.0 815.3 jit_solution(6109742581719975203)
XLA Ops:
  7.9 2.6 copy.29
  10.6 1.7 copy.32
  13.4 19.3 %all-gather.7.cloned.1.call-done = bf16[512,1664]{0,1:T(8,128)(2,1)} async-done(((bf16[512,416]{0,1:T(8,128)(2,1)}), bf16[512,1664]{0,1:T(8,128)(2,1)}) %all-gather.7.cloned.1.call-update) | async-done | bytes 1703952 | tf_op jit(solution)/shard_map/all_gather | solution.py:44
  32.7 2.7 copy.28
  36.1 104.4 %all-gather.9.cloned.1.call-done = bf16[1664,3,416]{2,1,0:T(4,128)(2,1)} async-done(((bf16[208,3,416]{2,1,0:T(4,128)(2,1)}), bf16[1664,3,416]{2,1,0:T(4,128)(2,1)}) %all-gather.9.cloned.1.call-update) | async-done | bytes 4153360 | tf_op jit(solution)/shard_map/all_gather | solution.py:48
  140.5 11.3 %copy.30 = bf16[1664,3,416]{0,2,1:T(8,128)(2,1)} copy(bf16[1664,3,416]{2,1,0:T(4,128)(2,1)} %all-gather.9.cloned.1.call-done) | data formatting | bytes 8306688 | tf_op jit(solution)/shard_map/all_gather | solution.py:48
  151.7 4.8 convolution_convert_fusion
  157.3 2.1 fusion.109
  160.0 26.7 %all-gather.11.cloned.1.call-done = bf16[416,1664]{0,1:T(8,128)(2,1)} async-done(((bf16[416,208]{0,1:T(8,128)(2,1)}), bf16[416,1664]{0,1:T(8,128)(2,1)}) %all-gather.11.cloned.1.call-update) | async-done | bytes 1384464 | tf_op jit(solution)/shard_map/all_gather | solution.py:60
  186.7 4.4 fusion.110
  192.5 70.4 %all-reduce.3.cloned.1.call-done = f32[512,1664]{1,0:T(8,128)} async-done(((f32[512,1664]{1,0:T(8,128)}), f32[512,1664]{1,0:T(8,128)}) %all-reduce.3.cloned.1.call-update) | async-done | bytes 3407888 | tf_op jit(solution)/shard_map/psum | solution.py:24
  262.9 2.7 convert_reduce_fusion
  265.6 105.1 %all-gather.13.cloned.1.call-done = bf16[1664,2048]{1,0:T(8,128)(2,1)} async-done(((bf16[208,2048]{1,0:T(8,128)(2,1)}), bf16[1664,2048]{1,0:T(8,128)(2,1)}) %all-gather.13.cloned.1.call-update) | async-done | bytes 6815760 | tf_op jit(solution)/shard_map/all_gather | solution.py:65
  370.6 105.8 %all-gather.15.cloned.1.call-done = bf16[2048,1664]{0,1:T(8,128)(2,1)} async-done(((bf16[2048,208]{0,1:T(8,128)(2,1)}), bf16[2048,1664]{0,1:T(8,128)(2,1)}) %all-gather.15.cloned.1.call-update) | async-done | bytes 6815760 | tf_op jit(solution)/shard_map/all_gather | solution.py:69
  476.5 21.5 %fusion.20 = f32[512,1664]{1,0:T(8,128)} fusion(bf16[2048,1664]{0,1:T(8,128)(2,1)} %all-gather.15.cloned.1.call-done, bf16[1664,2048]{1,0:T(8,128)(2,1)} %all-gather.13.cloned.1.call-done, bf16[512,1664]{1,0:T(8,128)(2,1)S(1)} %get-tuple-element.7, f32[512]{0:T(512)S(1)} %get-tuple-element.13, f32[512]{0:T(512)S(1)} %get-tuple-element.12), kind=kOutput, calls=%fused_computation.42 | convolution fusion | flops 7050887168 | bytes 18747392 | tf_op jit(solution)/shard_map/dot_general | solution.py:67
  499.2 69.8 %all-reduce.5.cloned.1.call-done = f32[512,1664]{1,0:T(8,128)} async-done(((f32[512,1664]{1,0:T(8,128)}), f32[512,1664]{1,0:T(8,128)}) %all-reduce.5.cloned.1.call-update) | async-done | bytes 3407888 | tf_op jit(solution)/shard_map/psum | solution.py:24
  569.0 2.2 fusion.18
  572.4 1.3 copy.35
  573.8 42.4 %psum.23 = f32[8]{0:T(128)S(1)} all-reduce(f32[8]{0:T(128)S(1)} %select_reduce_fusion.1), channel_id=1, replica_groups=mesh['gx'=4,'gy'=8] {'gx','gy'}, use_global_device_ids=true, to_apply=%region_11.12 | all-reduce | flops 8 | bytes 64 | tf_op jit(solution)/shard_map/psum | solution.py:87
  616.2 2.3 gather_fusion
  618.5 1.2 gather.7
  620.2 141.2 %all-gather.17.cloned.1.call-done = bf16[6656,1024]{1,0:T(8,128)(2,1)} async-done(((bf16[832,1024]{1,0:T(8,128)(2,1)}), bf16[6656,1024]{1,0:T(8,128)(2,1)}) %all-gather.17.cloned.1.call-update) | async-done | bytes 13631504 | tf_op jit(solution)/shard_map/all_gather | solution.py:85
  761.5 8.4 %fusion.108 = (f32[]{:T(128)}, bf16[128,1024]{1,0:T(8,128)(2,1)}) fusion(bf16[6656,1024]{1,0:T(8,128)(2,1)} %all-gather.17.cloned.1.call-done, pred[128,6656]{1,0:T(8,128)(4,1)} %bitcast.26, bf16[128,6656]{1,0:T(8,128)(2,1)S(1)} %gather.7), kind=kOutput, calls=%fused_computation.138 | convolution fusion | flops 1745944576 | bytes 16449540 | tf_op jit(solution)/shard_map/dot_general | solution.py:19
  769.9 38.6 %pmax.7 = f32[]{:T(128)} all-reduce(f32[]{:T(128)} %get-tuple-element.10), channel_id=1, replica_groups=mesh['gx'=4,'gy'=8] {'gx','gy'}, use_global_device_ids=true, to_apply=%region_13.14 | all-reduce | flops 1 | bytes 8 | tf_op jit(solution)/shard_map/pmax | solution.py:88
  (41 shorter events, 8.0 us)
Async XLA Ops:
  7.2 25.5 %all-gather.7.cloned.1.call-start = ((), (), s32[]{:S(2)}) async-start(), calls=%async_computation | async-start | bytes 2129920 | tf_op jit(solution)/shard_map/all_gather | solution.py:44
  7.9 132.6 %all-gather.9.cloned.1.call-start = ((), (), s32[]{:S(2)}) async-start(), calls=%async_computation.1 | async-start | bytes 7667712 | tf_op jit(solution)/shard_map/all_gather | solution.py:48
  10.6 176.1 %all-gather.11.cloned.1.call-start = ((), (), s32[]{:S(2)}) async-start(), calls=%async_computation.2 | async-start | bytes 1916928 | tf_op jit(solution)/shard_map/all_gather | solution.py:60
  12.4 250.5 %all-reduce.3.cloned.1.call-start = ((), (), s32[]{:S(2)}) async-start(), calls=%async_computation.3 | async-start | bytes 6815744 | tf_op jit(solution)/shard_map/psum | solution.py:24
  191.1 179.6 %all-gather.13.cloned.1.call-start = ((), (), s32[]{:S(2)}) async-start(), calls=%async_computation.4 | async-start | bytes 7667712 | tf_op jit(solution)/shard_map/all_gather | solution.py:65
  191.7 284.8 %all-gather.15.cloned.1.call-start = ((), (), s32[]{:S(2)}) async-start(), calls=%async_computation.5 | async-start | bytes 7667712 | tf_op jit(solution)/shard_map/all_gather | solution.py:69
  192.3 376.7 %all-reduce.5.cloned.1.call-start = ((), (), s32[]{:S(2)}) async-start(), calls=%async_computation.6 | async-start | bytes 6815744 | tf_op jit(solution)/shard_map/psum | solution.py:24
  497.9 0.8 copy-start.1
  497.9 1.2 copy-start.2
  498.0 263.5 %all-gather.17.cloned.1.call-start = ((), (), s32[]{:S(2)}) async-start(), calls=%async_computation.7 | async-start | bytes 15335424 | tf_op jit(solution)/shard_map/all_gather | solution.py:85
  498.7 72.9 %copy-start = (s32[512]{0:T(512)S(1)}, s32[512]{0:T(512)}, u32[]{:S(2)}) copy-start(s32[512]{0:T(512)} %param.10) | copy-start | bytes 6148
Sparse Core Ops, SparseCore 0:
  9.6 23.0 all-gather.6
  34.9 105.5 all-gather.8
  143.2 43.4 all-gather.10
  191.2 71.6 all-reduce.2
  264.9 105.6 all-gather.12
  372.7 103.7 all-gather.14
  498.1 70.8 all-reduce.4
  571.2 190.2 all-gather.16
where the time goes:
time: 816 us; the launch traced here: 815 us
  waiting for transfers between devices  645 us (79%)
  blocking collectives  81.1 us (10%)
  matrix products  40.3 us (5%)
  local copies, waits for them, and re-layouts  24.7 us (3%)
  between operations  14.3 us (2%)
  other arithmetic  9.36 us (1%)
    all_gather x1, waiting for transfers between devices, per_device(): lax.all_gather(merge_weight, 'gy', axis=0, tiled=True)  141 us
    psum x2, waiting for transfers between devices, finish_sum(): summed = lax.psum(head_partial, 'gx')  140 us
    all_gather x1, waiting for transfers between devices, per_device(): lax.all_gather(down_weight, 'gy', axis=1, tiled=True)  106 us
    all_gather x1, waiting for transfers between devices, per_device(): lax.all_gather(up_weight, 'gy', axis=0, tiled=True)  105 us
    all_gather x1, waiting for transfers between devices, per_device(): lax.all_gather(qkv_weight, 'gy', axis=0, tiled=True)  104 us
    psum x1, blocking collectives, per_device(): request_sq = lax.psum(request_part, ('gx', 'gy'))  42.4 us
    pmax x1, blocking collectives, per_device(): top_logit = lax.pmax(local_top, ('gx', 'gy'))  38.6 us
    all_gather x1, waiting for transfers between devices, per_device(): lax.all_gather(out_weight, 'gy', axis=1, tiled=True)  26.7 us
  transfers between devices with their start and end apart: 8, of which 8 were waited for; matrix products, arithmetic and copies ran while one was open for 5% of the time, Pallas kernels for 0%

commit v1 on v0

--- a/solution.py
+++ b/solution.py
@@ -21,7 +21,7 @@
 
 def finish_sum(head_partial, stream_full, feat_share):
     own_index = lax.axis_index("gx")
-    summed = lax.psum(head_partial, "gx")
+    summed = jnp.sum(lax.all_gather(head_partial, "gx"), axis=0)
     new_full = (stream_full.astype(jnp.float32) + summed).astype(jnp.bfloat16)
     new_share = lax.dynamic_slice_in_dim(new_full, own_index * feat_share, feat_share, 1)
     return (new_full, new_share)

time: 816 us -> 888 us (1.088)
  waiting for transfers between devices: 645 us -> 701 us
  other arithmetic: 9.36 us -> 25.6 us
    all_gather x0 -> x2, waiting for transfers between devices: none -> 169 us  [finish_sum(): summed = jnp.sum(lax.all_gather(head_partial, 'gx'), axis=0)]
    psum x2 -> x0, waiting for transfers between devices: 140 us -> none  [finish_sum(): summed = lax.psum(head_partial, 'gx')]
    all_gather x1, waiting for transfers between devices: 141 us -> 176 us  [per_device(): lax.all_gather(merge_weight, 'gy', axis=0, tiled=True)]
    reduce_sum x0 -> x2, other arithmetic: none -> 15.7 us  [finish_sum(): summed = jnp.sum(lax.all_gather(head_partial, 'gx'), axis=0)]
  transfers between devices with their start and end apart: 8 -> 8, of which waited for: 8 -> 8; matrix products, arithmetic and copies ran while one was open for 5% -> 6% of each run, Pallas kernels for 0% -> 0%
where the time goes in v1:
time: 888 us; the launch traced here: 887 us
  waiting for transfers between devices  701 us (79%)
  blocking collectives  79.5 us (9%)
  matrix products  41.1 us (5%)
  local copies, waits for them, and re-layouts  25.6 us (3%)
  other arithmetic  25.6 us (3%)
  between operations  14.2 us (2%)
    all_gather x1, waiting for transfers between devices, per_device(): lax.all_gather(merge_weight, 'gy', axis=0, tiled=True)  176 us
    all_gather x2, waiting for transfers between devices, finish_sum(): summed = jnp.sum(lax.all_gather(head_partial, 'gx'), axis=0)  169 us
    all_gather x1, waiting for transfers between devices, per_device(): lax.all_gather(down_weight, 'gy', axis=1, tiled=True)  106 us
    all_gather x1, waiting for transfers between devices, per_device(): lax.all_gather(qkv_weight, 'gy', axis=0, tiled=True)  104 us
    all_gather x1, waiting for transfers between devices, per_device(): lax.all_gather(up_weight, 'gy', axis=0, tiled=True)  96.9 us
    psum x1, blocking collectives, per_device(): request_sq = lax.psum(request_part, ('gx', 'gy'))  40.9 us
    pmax x1, blocking collectives, per_device(): top_logit = lax.pmax(local_top, ('gx', 'gy'))  38.6 us
    all_gather x1, waiting for transfers between devices, per_device(): lax.all_gather(out_weight, 'gy', axis=1, tiled=True)  26.8 us
  transfers between devices with their start and end apart: 8, of which 8 were waited for; matrix products, arithmetic and copies ran while one was open for 6% of the time, Pallas kernels for 0%

profile of v1, /device:TPU:0, one launch (start us, length us, event | category | flops | bytes accessed | tf_op | source)
XLA Modules:
  0.0 887.2 jit_solution(16623817258390330057)
XLA Ops:
  7.9 2.6 copy.29
  13.4 19.3 %all-gather.11.cloned.1.call-done = bf16[512,1664]{0,1:T(8,128)(2,1)} async-done(((bf16[512,416]{0,1:T(8,128)(2,1)}), bf16[512,1664]{0,1:T(8,128)(2,1)}) %all-gather.11.cloned.1.call-update) | async-done | bytes 1703952 | tf_op jit(solution)/shard_map/all_gather | solution.py:44
  32.7 2.7 copy.28
  36.1 104.4 %all-gather.13.cloned.1.call-done = bf16[1664,3,416]{2,1,0:T(4,128)(2,1)} async-done(((bf16[208,3,416]{2,1,0:T(4,128)(2,1)}), bf16[1664,3,416]{2,1,0:T(4,128)(2,1)}) %all-gather.13.cloned.1.call-update) | async-done | bytes 4153360 | tf_op jit(solution)/shard_map/all_gather | solution.py:48
  140.5 11.3 %copy.30 = bf16[1664,3,416]{0,2,1:T(8,128)(2,1)} copy(bf16[1664,3,416]{2,1,0:T(4,128)(2,1)} %all-gather.13.cloned.1.call-done) | data formatting | bytes 8306688 | tf_op jit(solution)/shard_map/all_gather | solution.py:48
  151.7 4.8 convolution_convert_fusion
  157.3 2.1 fusion.109
  159.9 26.8 %all-gather.15.cloned.1.call-done = bf16[416,1664]{0,1:T(8,128)(2,1)} async-done(((bf16[416,208]{0,1:T(8,128)(2,1)}), bf16[416,1664]{0,1:T(8,128)(2,1)}) %all-gather.15.cloned.1.call-update) | async-done | bytes 1384464 | tf_op jit(solution)/shard_map/all_gather | solution.py:60
  186.7 4.5 fusion.110
  192.7 85.8 %all-gather.23.cloned.1.call-done = f32[2048,1664]{1,0:T(8,128)} async-done(((f32[512,1664]{1,0:T(8,128)}), f32[2048,1664]{1,0:T(8,128)}) %all-gather.23.cloned.1.call-update) | async-done | bytes 13631504 | tf_op jit(solution)/shard_map/all_gather | solution.py:24
  278.4 7.8 reduce_sum.93
  286.3 2.9 convert_reduce_fusion
  289.2 96.9 %all-gather.17.cloned.1.call-done = bf16[1664,2048]{1,0:T(8,128)(2,1)} async-done(((bf16[208,2048]{1,0:T(8,128)(2,1)}), bf16[1664,2048]{1,0:T(8,128)(2,1)}) %all-gather.17.cloned.1.call-update) | async-done | bytes 6815760 | tf_op jit(solution)/shard_map/all_gather | solution.py:65
  386.1 105.8 %all-gather.19.cloned.1.call-done = bf16[2048,1664]{0,1:T(8,128)(2,1)} async-done(((bf16[2048,208]{0,1:T(8,128)(2,1)}), bf16[2048,1664]{0,1:T(8,128)(2,1)}) %all-gather.19.cloned.1.call-update) | async-done | bytes 6815760 | tf_op jit(solution)/shard_map/all_gather | solution.py:69
  491.9 21.6 %fusion.20 = f32[512,1664]{1,0:T(8,128)} fusion(bf16[2048,1664]{0,1:T(8,128)(2,1)} %all-gather.19.cloned.1.call-done, bf16[1664,2048]{1,0:T(8,128)(2,1)} %all-gather.17.cloned.1.call-done, bf16[512,1664]{1,0:T(8,128)(2,1)S(1)} %get-tuple-element.7, f32[512]{0:T(512)S(1)} %get-tuple-element.13, f32[512]{0:T(512)S(1)} %get-tuple-element.12), kind=kOutput, calls=%fused_computation.42 | convolution fusion | flops 7050887168 | bytes 18747392 | tf_op jit(solution)/shard_map/dot_general | solution.py:67
  516.6 83.4 %all-gather.25.cloned.1.call-done = f32[2048,1664]{1,0:T(8,128)} async-done(((f32[512,1664]{1,0:T(8,128)}), f32[2048,1664]{1,0:T(8,128)}) %all-gather.25.cloned.1.call-update) | async-done | bytes 13631504 | tf_op jit(solution)/shard_map/all_gather | solution.py:24
  600.0 7.8 reduce_sum.96
  607.8 2.6 fusion.18
  610.4 2.3 gather_fusion
  612.7 2.1 gather.7
  615.5 175.9 %all-gather.21.cloned.1.call-done = bf16[6656,1024]{1,0:T(8,128)(2,1)} async-done(((bf16[832,1024]{1,0:T(8,128)(2,1)}), bf16[6656,1024]{1,0:T(8,128)(2,1)}) %all-gather.21.cloned.1.call-update) | async-done | bytes 13631504 | tf_op jit(solution)/shard_map/all_gather | solution.py:85
  791.4 8.9 %fusion.108 = (f32[]{:T(128)}, bf16[128,1024]{1,0:T(8,128)(2,1)}) fusion(bf16[6656,1024]{1,0:T(8,128)(2,1)} %all-gather.21.cloned.1.call-done, pred[128,6656]{1,0:T(8,128)(4,1)} %bitcast.30, bf16[128,6656]{1,0:T(8,128)(2,1)} %gather.7), kind=kOutput, calls=%fused_computation.138 | convolution fusion | flops 1745944576 | bytes 16449540 | tf_op jit(solution)/shard_map/dot_general | solution.py:19
  800.3 38.6 %pmax.7 = f32[]{:T(128)} all-reduce(f32[]{:T(128)} %get-tuple-element.10), channel_id=1, replica_groups=mesh['gx'=4,'gy'=8] {'gx','gy'}, use_global_device_ids=true, to_apply=%region_13.14 | all-reduce | flops 1 | bytes 8 | tf_op jit(solution)/shard_map/pmax | solution.py:88
  838.9 40.9 %psum.7 = f32[8]{0:T(128)S(1)} all-reduce(f32[8]{0:T(128)S(1)} %select_reduce_fusion.1), channel_id=1, replica_groups=mesh['gx'=4,'gy'=8] {'gx','gy'}, use_global_device_ids=true, to_apply=%region_11.12 | all-reduce | flops 8 | bytes 64 | tf_op jit(solution)/shard_map/psum | solution.py:87
  (43 shorter events, 11.0 us)
Async XLA Ops:
  7.2 25.5 %all-gather.11.cloned.1.call-start = ((), (), s32[]{:S(2)}) async-start(), calls=%async_computation | async-start | bytes 2129920 | tf_op jit(solution)/shard_map/all_gather | solution.py:44
  7.9 132.6 %all-gather.13.cloned.1.call-start = ((), (), s32[]{:S(2)}) async-start(), calls=%async_computation.1 | async-start | bytes 7667712 | tf_op jit(solution)/shard_map/all_gather | solution.py:48
  10.6 176.1 %all-gather.15.cloned.1.call-start = ((), (), s32[]{:S(2)}) async-start(), calls=%async_computation.2 | async-start | bytes 1916928 | tf_op jit(solution)/shard_map/all_gather | solution.py:60
  12.4 266.0 %all-gather.23.cloned.1.call-start = ((), (), s32[]{:S(2)}) async-start(), calls=%async_computation.6 | async-start | bytes 17039360 | tf_op jit(solution)/shard_map/all_gather | solution.py:24
  191.3 194.8 %all-gather.17.cloned.1.call-start = ((), (), s32[]{:S(2)}) async-start(), calls=%async_computation.3 | async-start | bytes 7667712 | tf_op jit(solution)/shard_map/all_gather | solution.py:65
  191.9 300.0 %all-gather.19.cloned.1.call-start = ((), (), s32[]{:S(2)}) async-start(), calls=%async_computation.4 | async-start | bytes 7667712 | tf_op jit(solution)/shard_map/all_gather | solution.py:69
  192.4 407.5 %all-gather.25.cloned.1.call-start = ((), (), s32[]{:S(2)}) async-start(), calls=%async_computation.7 | async-start | bytes 17039360 | tf_op jit(solution)/shard_map/all_gather | solution.py:24
  513.5 0.8 copy-start.1
  513.5 3.0 copy-start.2
  513.5 277.9 %all-gather.21.cloned.1.call-start = ((), (), s32[]{:S(2)}) async-start(), calls=%async_computation.5 | async-start | bytes 15335424 | tf_op jit(solution)/shard_map/all_gather | solution.py:85
  610.4 4.8 copy-start
Sparse Core Ops, SparseCore 0:
  9.6 23.0 all-gather.10
  34.9 105.5 all-gather.12
  143.2 43.4 all-gather.14
  191.4 86.9 all-gather.22
  280.5 105.5 all-gather.16
  388.1 103.7 all-gather.18
  513.7 86.2 all-gather.24
  602.2 189.2 all-gather.20
